TPU v7x, 256 devices: a whole 4x4x8 slice. The times are simulated.
256 devices in a mesh: space: 8 (over z_lo, y), vec: 32 (over x, z_hi, core).
Axes of the slice: x: 4, y: 4, z: 8 (z_hi: 4, z_lo: 2; z = z_hi * 2 + z_lo), core: 2. Of those that a mesh axis runs over, the one named last changes fastest.
Arguments:
- vectors: float32 [2, 3, 128, 8, 4096], P(None, None, 'vec', 'space'), may hold values from -6 to 6
- gauge_links: float32 [3, 2, 3, 3, 8, 4096], P(None, None, None, None, 'space'), may hold values from -2.5 to 2.5
- momenta: int32 [2, 3], replicated, may hold values from 1 to 2
- displacements: int32 [2], replicated, may hold values from 0 to 5
Outputs:
- elementals: float32 [2, 4, 128, 128], P(None, None, 'vec', 'space')
All inputs are finite; a program needn't handle non-finite values.
Results may differ from a plain program's by a relative error of at most 0.0003.
Values sent between devices are 32-bit elements; how exact they have to be, the bound alone decides.
No kernel may reach another device: no remote copies, remote signals or barrier semaphores. Data moves between devices by JAX's collectives and lax.ppermute only.
A program may use at most 128 MiB of HBM per device.

v0:
```python
import math
import jax
import jax.numpy as jnp
from jax import lax
from jax.sharding import PartitionSpec as P

NY = 64
NZ = 64
NMOM = 2
NDISP = 2


def extended(block, sides, width):
    for axis, dim in sides:
        count = lax.axis_size(axis)
        forward = [(i, i + 1) for i in range(count - 1)]
        forward.append((count - 1, 0))
        backward = [(target, source) for source, target in forward]
        low = lax.ppermute(
            lax.slice_in_dim(block, block.shape[dim] - width, None, axis=dim), axis, forward
        )
        high = lax.ppermute(lax.slice_in_dim(block, 0, width, axis=dim), axis, backward)
        block = jnp.concatenate([low, block, high], axis=dim)
    return block


def shifted(block, axis, distance):
    devices = range(lax.axis_size(axis))
    route = [((i - distance) % len(devices), i) for i in devices]
    return lax.ppermute(block, axis, route)


def colour_term(gauge_one, colour_field, colour, dagger):
    if dagger:
        link_re = gauge_one[0][colour][:, None]
        link_im = -gauge_one[1][colour][:, None]
    else:
        link_re = gauge_one[0][:, colour][:, None]
        link_im = gauge_one[1][:, colour][:, None]
    vec_re = colour_field[0][colour][None]
    vec_im = colour_field[1][colour][None]
    return (link_re * vec_re - link_im * vec_im, link_re * vec_im + link_im * vec_re)


def link_times(gauge_one, colour_field, dagger):
    real_sum, imag_sum = colour_term(gauge_one, colour_field, 0, dagger)
    for colour in (1, 2):
        real_next, imag_next = colour_term(gauge_one, colour_field, colour, dagger)
        real_sum = real_sum + real_next
        imag_sum = imag_sum + imag_next
    return jnp.stack([real_sum, imag_sum])


def roll_depth(colour_field, offset, row_len):
    total_len = colour_field.shape[-1]
    position = lax.broadcasted_iota(jnp.int32, (total_len,), 0) % row_len
    if offset > 0:
        inner_roll = jnp.roll(colour_field, -1, -1)
        outer_roll = jnp.roll(colour_field, row_len - 1, -1)
        return jnp.where(position == row_len - 1, outer_roll, inner_roll)
    inner_roll = jnp.roll(colour_field, 1, -1)
    outer_roll = jnp.roll(colour_field, 1 - row_len, -1)
    return jnp.where(position == 0, outer_roll, inner_roll)


def plane_pair(colour_field):
    padded = extended(colour_field, (("space", 3),), 1)
    return (padded[:, :, :, 2:], padded[:, :, :, :-2])


def slab_neighbours(colour_field):
    return (
        plane_pair(colour_field),
        (jnp.roll(colour_field, -NZ, 4), jnp.roll(colour_field, NZ, 4)),
        (roll_depth(colour_field, 1, NZ), roll_depth(colour_field, -1, NZ)),
    )


def six_hops(gauge_sites, gauge_back, neighbours):
    forward = [
        link_times(gauge_sites[direction], neighbours[direction][0], False)
        for direction in range(3)
    ]
    backward = [
        link_times(gauge_back[direction], neighbours[direction][1], True) for direction in range(3)
    ]
    return forward + backward


def hopping_sum(hop_list):
    running = hop_list[0]
    for hop_index in range(1, 6):
        running = running + hop_list[hop_index]
    return running


def pair_sums(left_side, right_side):
    hig = lax.Precision.HIGHEST
    real_part = jnp.einsum(
        "cixs,cjxs->ij", left_side[0], right_side[0], precision=hig
    ) + jnp.einsum("cixs,cjxs->ij", left_side[1], right_side[1], precision=hig)
    imag_part = jnp.einsum(
        "cixs,cjxs->ij", left_side[0], right_side[1], precision=hig
    ) - jnp.einsum("cixs,cjxs->ij", left_side[1], right_side[0], precision=hig)
    return (real_part, imag_part)


def local(vectors, gauge_links, momenta, displacements):
    planes = vectors.shape[3]
    global_planes = planes * lax.axis_size("space")
    edge_plane = shifted(gauge_links[0], "space", 1)
    back_plane = jnp.concatenate([edge_plane, gauge_links[0][:, :, :, :-1, :]], 3)
    back_row = jnp.roll(gauge_links[1], NZ, 4)
    back_depth = roll_depth(gauge_links[2], -1, NZ)
    gauge_back = jnp.stack([back_plane, back_row, back_depth])
    first_step = hopping_sum(six_hops(gauge_links, gauge_back, slab_neighbours(vectors))) / -6.0
    filtered = (
        hopping_sum(six_hops(gauge_links, gauge_back, slab_neighbours(first_step))) / -3.0 - vectors
    )
    slab_hops = jnp.stack(six_hops(gauge_links, gauge_back, slab_neighbours(filtered)))
    chosen = [
        lax.dynamic_index_in_dim(slab_hops, displacements[op_index], 0, False)
        for op_index in range(NDISP)
    ]
    exchanged = lax.all_to_all(
        jnp.stack([filtered] + chosen), "vec", split_axis=5, concat_axis=3, tiled=True
    )
    block_field = exchanged[0]
    displaced = [exchanged[1 + op_index] for op_index in range(NDISP)]
    block_len = block_field.shape[4]
    plane_index = lax.axis_index("space") * planes + jnp.arange(planes, dtype=jnp.int32)
    flat_index = lax.axis_index("vec") * block_len + jnp.arange(block_len, dtype=jnp.int32)
    row_index = flat_index // NZ
    depth_index = flat_index % NZ
    real_rows = []
    imag_rows = []
    for op_index in range(NMOM):
        phase_plane = (momenta[op_index, 0] * plane_index % global_planes).astype(
            jnp.float32
        ) / global_planes
        phase_row = (momenta[op_index, 1] * row_index % NY).astype(jnp.float32) / NY
        phase_depth = (momenta[op_index, 2] * depth_index % NZ).astype(jnp.float32) / NZ
        angle_grid = (phase_plane[:, None] + phase_row[None, :] + phase_depth[None, :]) * (
            2.0 * math.pi
        )
        cosine = jnp.cos(angle_grid)
        sine_part = jnp.sin(angle_grid)
        phased = jnp.stack(
            [
                cosine * block_field[0] - sine_part * block_field[1],
                cosine * block_field[1] + sine_part * block_field[0],
            ]
        )
        real_part, imag_part = pair_sums(block_field, phased)
        real_rows.append(real_part)
        imag_rows.append(imag_part)
    for op_index in range(NDISP):
        real_part, imag_part = pair_sums(block_field, displaced[op_index])
        real_rows.append(real_part)
        imag_rows.append(imag_part)
    partial_sums = jnp.stack([jnp.stack(real_rows), jnp.stack(imag_rows)])
    share_sums = lax.psum_scatter(partial_sums, "vec", scatter_dimension=2, tiled=True)
    whole_sums = lax.psum_scatter(share_sums, "space", scatter_dimension=3, tiled=True)
    norm_scale = 1.0 / math.sqrt(3 * global_planes * NY * NZ)
    return whole_sums * norm_scale


def solution(mesh):
    placed = (
        P(None, None, "vec", "space", None),
        P(None, None, None, None, "space", None),
        P(),
        P(),
    )
    return jax.shard_map(
        local, mesh=mesh, in_specs=placed, out_specs=P(None, None, "vec", "space"), check_vma=False
    )
```

profile of v0, /device:TPU:2, one launch (start us, length us, event | category | flops | bytes accessed | tf_op | source)
XLA Modules:
  0.0 637.9 jit_solution(12803463155827763475)
XLA Ops:
  6.5 1.6 collective-permute-start.2
  8.1 2.8 collective-permute-start
  10.9 1.9 slice_bitcast_fusion.1
  12.8 2.1 fusion.117
  15.0 0.9 fusion.120
  15.9 0.9 fusion.123
  17.9 3.8 broadcast_select_fusion.2
  22.7 0.7 broadcast_select_fusion.6
  23.9 0.7 fusion.62
  24.8 0.9 fusion.52
  26.9 1.1 add_bitcast_fusion.15
  28.1 1.1 add_bitcast_fusion.19
  29.2 1.1 add_bitcast_fusion.21
  30.3 1.9 add_bitcast_fusion.13
  32.2 0.7 fusion.132
  36.1 0.8 copy.552
  37.0 0.8 copy.553
  37.8 0.8 copy.554
  38.7 0.8 copy.555
  39.5 0.8 copy.557
  41.7 1.1 fusion.126
  43.0 1.0 fusion.118
  44.3 1.0 fusion.124
  45.7 1.3 add_bitcast_fusion.17
  47.0 1.1 add_bitcast_fusion.23
  48.1 1.9 fusion.18
  50.0 0.8 fusion.19
  50.8 4.1 collective-permute-start.3
  54.9 0.9 fusion.107
  55.9 0.9 fusion.110
  56.8 0.9 fusion.113
  59.2 0.9 broadcast_select_fusion.4
  60.4 0.9 fusion.42
  61.6 0.9 broadcast_select_fusion.1
  62.9 1.1 add_bitcast_fusion.9
  64.0 1.1 add_bitcast_fusion.7
  65.1 1.1 add_bitcast_fusion.3
  66.3 1.1 add_bitcast_fusion.1
  67.8 2.8 collective-permute-done.4
  70.9 1.1 add_bitcast_fusion.11
  72.0 1.3 add_bitcast_fusion.5
  73.3 2.2 fusion.30
  76.1 0.9 fusion.98
  77.0 0.9 fusion.99
  78.0 0.9 fusion.102
  79.1 4.1 collective-permute-start.5
  83.2 0.9 broadcast_select_fusion
  84.5 0.9 fusion.32
  85.7 0.9 broadcast_select_fusion.3
  89.2 1.0 collective-permute-done.6
  92.7 33.3 %copy.147 = f32[3,2,3,4,1,4096]{3,2,4,1,0,5:T(4,128)} copy(f32[3,2,3,4,1,4096]{5,3,2,1,4,0:T(4,128)S(1)} %pad_maximum_fusion) | data formatting | bytes 2359296 | tf_op jit(solution)/shard_map/stack | solution.py:126
  126.0 40.0 %reshape.3120 = f32[32,1,9216]{2,1,0:T(1,128)} reshape(f32[4096,3,2,1,3,4]{5,4,3,2,1,0:T(4,128)} %bitcast.634) | data formatting | bytes 2359296
  166.0 11.0 %all-to-all-start = ((f32[32,1,9216]{2,1,0:T(1,128)}), f32[32,1,9216]{2,1,0:T(1,128)S(1)}, u32[]{:S(2)}, u32[]{:S(2)}) async-start(f32[32,1,9216]{2,1,0:T(1,128)} %reshape.3120), calls=%async_computation | async-start | bytes 2359296 | tf_op jit(solution)/shard_map/all_to_all | solution.py:125
  179.3 2.7 fusion.92
  182.0 25.1 %all-to-all-done = f32[32,1,9216]{2,1,0:T(1,128)S(1)} async-done(((f32[32,1,9216]{2,1,0:T(1,128)}), f32[32,1,9216]{2,1,0:T(1,128)S(1)}, u32[]{:S(2)}, u32[]{:S(2)}) %all-to-all-start) | async-done | bytes 1179680 | tf_op jit(solution)/shard_map/all_to_all | solution.py:125
  207.6 3.4 reduce
  211.1 50.4 %reshape.3121 = f32[4096,3,2,1,3,4]{5,4,3,2,1,0:T(4,128)} reshape(f32[32,9216]{1,0:T(8,128)S(1)} %reduce) | data formatting | bytes 2359296
  261.5 36.2 %copy.148 = f32[3,2,3,4,1,4096]{5,4,3,2,1,0:T(1,128)S(1)} copy(f32[3,2,3,4,1,4096]{3,2,4,1,0,5:T(4,128)} %bitcast.635) | data formatting | bytes 2359296 | tf_op jit(solution)/shard_map/all_to_all | solution.py:125
  305.6 0.8 pad_maximum_fusion.1
  307.7 268.2 %all-reduce.3.cloned.1.call-done = f32[2,4,128,128]{3,2,1,0:T(8,128)} async-done(((f32[2,4,128,128]{3,2,1,0:T(8,128)}), f32[2,4,128,128]{3,2,1,0:T(8,128)}) %all-reduce.3.cloned.1.call-update) | async-done | bytes 524304
  575.9 0.8 constant_dynamic-slice_fusion
  577.0 1.0 reshape.3117
  577.9 51.2 %reduce-scatter.5.cloned.1.call-done = f32[16,32]{1,0:T(8,128)} async-done(((f32[128,32]{1,0:T(8,128)}), f32[16,32]{1,0:T(8,128)}) %reduce-scatter.5.cloned.1.call-update) | async-done | bytes 2064
  629.1 0.8 reshape.3118
  (230 shorter events, 25.5 us)
Async XLA Ops:
  6.5 8.4 %copy-start = (f32[2,3,4,1,4096]{4,3,2,1,0:T(1,128)S(1)}, f32[2,3,4,1,4096]{4,3,2,1,0:T(1,128)}, u32[]{:S(2)}) copy-start(f32[2,3,4,1,4096]{4,3,2,1,0:T(1,128)} %param.4) | copy-start | bytes 1179652
  6.5 36.5 %collective-permute-start.2 = (f32[2,3,4,1,4096]{4,3,2,1,0:T(1,128)}, f32[2,3,4,1,4096]{4,3,2,1,0:T(1,128)}, u32[]{:S(2)}, u32[]{:S(2)}) collective-permute-start(f32[2,3,4,1,4096]{4,3,2,1,0:T(1,128)} %param.4), channel_id=1, source_target_pairs={{0,32},{32,64},{64,96},{96,128},{128,160},{160,192},{192,224},{224... | collective-permute-start | bytes 1179656 | tf_op jit(solution)/shard_map/ppermute | solution.py:19
  8.1 36.2 %collective-permute-start = (f32[2,3,4,1,4096]{4,3,2,1,0:T(1,128)}, f32[2,3,4,1,4096]{4,3,2,1,0:T(1,128)}, u32[]{:S(2)}, u32[]{:S(2)}) collective-permute-start(f32[2,3,4,1,4096]{4,3,2,1,0:T(1,128)} %param.4), channel_id=1, source_target_pairs={{32,0},{64,32},{96,64},{128,96},{160,128},{192,160},{224,192},{0,2... | collective-permute-start | bytes 1179656 | tf_op jit(solution)/shard_map/ppermute | solution.py:22
  12.8 4.2 copy-start.1
  12.8 28.8 %collective-permute-start.1 = (f32[2,3,3,1,4096]{4,3,2,1,0:T(1,128)}, f32[2,3,3,1,4096]{4,3,2,1,0:T(1,128)}, u32[]{:S(2)}, u32[]{:S(2)}) collective-permute-start(f32[2,3,3,1,4096]{4,3,2,1,0:T(1,128)} %get-tuple-element.24), channel_id=1, source_target_pairs={{224,0},{0,32},{32,64},{64,96},{96,128},{128,160},{160,192},{192,2... | collective-permute-start | bytes 884744 | tf_op jit(solution)/shard_map/ppermute | solution.py:30
  28.1 4.8 copy-start.5
  45.6 4.4 copy-start.2
  45.7 4.4 copy-start.3
  50.8 16.6 %collective-permute-start.3 = (f32[2,3,4,1,4096]{4,3,2,1,0:T(1,128)S(1)}, f32[2,3,4,1,4096]{4,3,2,1,0:T(1,128)S(1)}, u32[]{:S(2)}, u32[]{:S(2)}) collective-permute-start(f32[2,3,4,1,4096]{4,3,2,1,0:T(1,128)S(1)} %fusion.19), channel_id=1, source_target_pairs={{32,0},{64,32},{96,64},{128,96},{160,128},{192,160},{224,192},{0,2... | collective-permute-start | bytes 1179656 | tf_op jit(solution)/shard_map/ppermute | solution.py:22
  57.8 12.7 %collective-permute-start.4 = (f32[2,3,4,1,4096]{4,3,2,1,0:T(1,128)S(1)}, f32[2,3,4,1,4096]{4,3,2,1,0:T(1,128)S(1)}, u32[]{:S(2)}, u32[]{:S(2)}) collective-permute-start(f32[2,3,4,1,4096]{4,3,2,1,0:T(1,128)S(1)} %fusion.19), channel_id=1, source_target_pairs={{0,32},{32,64},{64,96},{96,128},{128,160},{160,192},{192,224},{224... | collective-permute-start | bytes 1179656 | tf_op jit(solution)/shard_map/ppermute | solution.py:19
  79.0 11.3 %collective-permute-start.6 = (f32[2,3,4,1,4096]{4,3,2,1,0:T(1,128)S(1)}, f32[2,3,4,1,4096]{4,3,2,1,0:T(1,128)S(1)}, u32[]{:S(2)}, u32[]{:S(2)}) collective-permute-start(f32[2,3,4,1,4096]{4,3,2,1,0:T(1,128)S(1)} %copy_subtract_fusion), channel_id=1, source_target_pairs={{0,32},{32,64},{64,96},{96,128},{128,160},{160,192},{192,224},{224... | collective-permute-start | bytes 1179656 | tf_op jit(solution)/shard_map/ppermute | solution.py:19
  79.1 11.5 %collective-permute-start.5 = (f32[2,3,4,1,4096]{4,3,2,1,0:T(1,128)S(1)}, f32[2,3,4,1,4096]{4,3,2,1,0:T(1,128)S(1)}, u32[]{:S(2)}, u32[]{:S(2)}) collective-permute-start(f32[2,3,4,1,4096]{4,3,2,1,0:T(1,128)S(1)} %copy_subtract_fusion), channel_id=1, source_target_pairs={{32,0},{64,32},{96,64},{128,96},{160,128},{192,160},{224,192},{0,2... | collective-permute-start | bytes 1179656 | tf_op jit(solution)/shard_map/ppermute | solution.py:22
  166.0 11.2 %copy-start.4 = (s32[2,3]{1,0:T(2,128)S(1)}, s32[2,3]{1,0:T(2,128)}, u32[]{:S(2)}) copy-start(s32[2,3]{1,0:T(2,128)} %param.6) | copy-start | bytes 76
  166.0 41.1 %all-to-all-start = ((f32[32,1,9216]{2,1,0:T(1,128)}), f32[32,1,9216]{2,1,0:T(1,128)S(1)}, u32[]{:S(2)}, u32[]{:S(2)}) async-start(f32[32,1,9216]{2,1,0:T(1,128)} %reshape.3120), calls=%async_computation | async-start | bytes 2359296 | tf_op jit(solution)/shard_map/all_to_all | solution.py:125
  177.0 398.9 %all-reduce.3.cloned.1.call-start = ((), (), s32[]{:S(2)}) async-start(), calls=%async_computation.3 | async-start | bytes 1048576
  303.9 2.5 copy-start.6
  306.4 322.7 %reduce-scatter.5.cloned.1.call-start = ((), (), s32[]{:S(2)}) async-start(), calls=%async_computation.2 | async-start | bytes 73728
Sparse Core Ops, SparseCore 0:
  306.5 269.3 all-reduce.2
  578.5 50.5 reduce-scatter.4
where the time goes:
time: 646 us; the launch traced here: 638 us
  waiting for transfers between devices  348 us (54%)
  local copies, waits for them, and re-layouts  193 us (30%)
  other arithmetic  44.6 us (7%)
  starting transfers between devices  24.5 us (4%)
  between operations  21.3 us (3%)
    unnamed x4, waiting for transfers between devices  319 us
    unnamed x146, local copies, waits for them, and re-layouts  104 us
    all_to_all x2, local copies, waits for them, and re-layouts, local(): lax.all_to_all(jnp.stack([filtered] + chosen), 'vec', split_axis=5, conca...  36.7 us
    another operation x1, local copies, waits for them, and re-layouts, local(): jnp.stack([filtered] + chosen)  33.3 us
    all_to_all x1, waiting for transfers between devices, local(): lax.all_to_all(jnp.stack([filtered] + chosen), 'vec', split_axis=5, conca...  25.1 us
    another operation x12, other arithmetic, link_times(): return jnp.stack([real_sum, imag_sum])  14.6 us
  transfers between devices with their start and end apart: 10, of which 5 were waited for; matrix products, arithmetic and copies ran while one was open for 8% of the time, Pallas kernels for 0%

commit v1 on v0

--- a/solution.py
+++ b/solution.py
@@ -122,8 +122,9 @@
         lax.dynamic_index_in_dim(slab_hops, displacements[op_index], 0, False)
         for op_index in range(NDISP)
     ]
-    exchanged = lax.all_to_all(
-        jnp.stack([filtered] + chosen), "vec", split_axis=5, concat_axis=3, tiled=True
+    x_in = jnp.stack([filtered] + chosen)
+    exchanged = jnp.concatenate(
+        lax.all_to_all(jnp.stack(jnp.split(x_in, lax.axis_size("vec"), 5), 0), "vec", 0, 0), 3
     )
     block_field = exchanged[0]
     displaced = [exchanged[1 + op_index] for op_index in range(NDISP)]

time: 646 us -> 472 us (0.73)
  local copies, waits for them, and re-layouts: 193 us -> 41.9 us
  other arithmetic: 44.6 us -> 19.3 us
  waiting for transfers between devices: 348 us -> 357 us
    unnamed x146 -> x98, local copies, waits for them, and re-layouts: 104 us -> 27.4 us
    all_to_all x2 -> x1, local copies, waits for them, and re-layouts: 36.7 us -> 0.21 us  [local(): lax.all_to_all(jnp.stack(jnp.split(x_in, lax.axis_size('vec'), 5), 0), 'v...]
    another operation x1, local copies, waits for them, and re-layouts: 33.3 us -> 0.61 us  [local(): jnp.stack(jnp.split(x_in, lax.axis_size('vec'), 5), 0)]
    another operation x12, other arithmetic: 14.6 us -> 4.19 us  [link_times(): return jnp.stack([real_sum, imag_sum])]
  transfers between devices with their start and end apart: 10 -> 10, of which waited for: 5 -> 5; matrix products, arithmetic and copies ran while one was open for 8% -> 6% of each run, Pallas kernels for 0% -> 0%
where the time goes in v1:
time: 472 us; the launch traced here: 469 us
  waiting for transfers between devices  357 us (76%)
  local copies, waits for them, and re-layouts  41.9 us (9%)
  starting transfers between devices  24.4 us (5%)
  between operations  20.2 us (4%)
  other arithmetic  19.3 us (4%)
  matrix products  6.2 us (1%)
    unnamed x4, waiting for transfers between devices  320 us
    unnamed x98, local copies, waits for them, and re-layouts  27.4 us
    all_to_all x1, waiting for transfers between devices, local(): lax.all_to_all(jnp.stack(jnp.split(x_in, lax.axis_size('vec'), 5), 0), 'v...  25.6 us
    all_to_all x1, starting transfers between devices, local(): lax.all_to_all(jnp.stack(jnp.split(x_in, lax.axis_size('vec'), 5), 0), 'v...  10.9 us
    ppermute x3, starting transfers between devices, extended(): lax.ppermute(lax.slice_in_dim(block, 0, width, axis=dim), axis, backward)  9.81 us
  transfers between devices with their start and end apart: 10, of which 5 were waited for; matrix products, arithmetic and copies ran while one was open for 6% of the time, Pallas kernels for 0%

profile of v1, /device:TPU:2, one launch (start us, length us, event | category | flops | bytes accessed | tf_op | source)
XLA Modules:
  0.0 469.1 jit_solution(110087936946280246)
XLA Ops:
  6.5 1.6 collective-permute-start.2
  8.1 2.8 collective-permute-start
  10.9 1.9 slice_bitcast_fusion
  13.3 0.7 slice.1531
  14.1 0.9 fusion.140
  15.0 0.9 fusion.139
  16.0 0.9 fusion.143
  17.1 0.7 broadcast_select_fusion
  20.6 0.7 fusion.90
  21.5 0.9 fusion.36
  24.3 1.0 add_bitcast_fusion.19
  25.3 0.6 fusion.152
  29.1 0.8 copy.441
  31.2 1.1 fusion.147
  32.5 1.0 fusion.144
  33.8 1.0 fusion.145
  37.8 0.8 collective-permute-start.4
  38.6 3.4 collective-permute-start.3
  44.3 6.3 %collective-permute-done.4 = f32[2,3,4,1,4096]{4,2,1,0,3:T(4,128)S(1)} collective-permute-done((f32[2,3,4,1,4096]{4,2,1,0,3:T(4,128)S(1)}, f32[2,3,4,1,4096]{4,2,1,0,3:T(4,128)S(1)}, u32[]{:S(2)}, u32[]{:S(2)}) %collective-permute-start.4) | collective-permute-done | bytes 393248 | tf_op jit(solution)/shard_map/ppermute | solution.py:19
  51.2 0.7 fusion.188
  51.9 0.7 fusion.28
  53.7 0.7 collective-permute-start.6
  54.4 3.6 collective-permute-start.5
  60.2 4.7 %collective-permute-done.5 = f32[2,3,4,1,4096]{4,2,1,0,3:T(4,128)S(1)} collective-permute-done((f32[2,3,4,1,4096]{4,2,1,0,3:T(4,128)S(1)}, f32[2,3,4,1,4096]{4,2,1,0,3:T(4,128)S(1)}, u32[]{:S(2)}, u32[]{:S(2)}) %collective-permute-start.5) | collective-permute-done | bytes 393248 | tf_op jit(solution)/shard_map/ppermute | solution.py:22
  67.0 0.6 constant_dynamic-update-slice_fusion.31
  67.6 0.6 constant_dynamic-update-slice_fusion.30
  68.2 0.6 constant_dynamic-update-slice_fusion.29
  68.9 0.6 constant_dynamic-update-slice_fusion.28
  69.5 0.6 constant_dynamic-update-slice_fusion.27
  70.1 0.6 constant_dynamic-update-slice_fusion.26
  70.7 0.6 constant_dynamic-update-slice_fusion.25
  71.3 0.6 constant_dynamic-update-slice_fusion.24
  71.9 0.6 constant_dynamic-update-slice_fusion.23
  73.2 0.6 constant_dynamic-update-slice_fusion.21
  73.8 0.6 constant_dynamic-update-slice_fusion.20
  74.4 0.6 constant_dynamic-update-slice_fusion.19
  75.6 0.6 constant_dynamic-update-slice_fusion.17
  76.2 0.6 constant_dynamic-update-slice_fusion.16
  76.9 0.6 constant_dynamic-update-slice_fusion.15
  77.5 0.6 constant_dynamic-update-slice_fusion.14
  78.1 0.6 constant_dynamic-update-slice_fusion.13
  78.7 0.6 constant_dynamic-update-slice_fusion.12
  79.9 0.6 constant_dynamic-update-slice_fusion.10
  80.5 0.6 constant_dynamic-update-slice_fusion.9
  81.2 0.6 constant_dynamic-update-slice_fusion.8
  81.8 0.6 constant_dynamic-update-slice_fusion.7
  82.4 0.6 constant_dynamic-update-slice_fusion.6
  83.0 0.6 constant_dynamic-update-slice_fusion.5
  83.6 0.6 constant_dynamic-update-slice_fusion.4
  84.2 0.6 constant_dynamic-update-slice_fusion.3
  84.8 0.6 constant_dynamic-update-slice_fusion.2
  85.5 0.6 constant_dynamic-update-slice_fusion.1
  86.1 0.6 constant_dynamic-update-slice_fusion
  86.7 10.9 %all-to-all-start = ((f32[32,3,2,3,4,1,128]{6,5,4,3,2,1,0:T(1,128)}), f32[32,3,2,3,4,1,128]{6,5,4,3,2,1,0:T(1,128)S(1)}, u32[]{:S(2)}, u32[]{:S(2)}) async-start(f32[32,3,2,3,4,1,128]{6,5,4,3,2,1,0:T(1,128)} %constant_dynamic-update-slice_fusion), calls=%async_computation | async-start | bytes 2359296 | tf_op jit(solution)/shard_map/all_to_all | solution.py:127
  97.7 0.6 fusion.154
  99.6 2.4 fusion.120
  102.2 25.6 %all-to-all-done = f32[32,3,2,3,4,1,128]{6,5,4,3,2,1,0:T(1,128)S(1)} async-done(((f32[32,3,2,3,4,1,128]{6,5,4,3,2,1,0:T(1,128)}), f32[32,3,2,3,4,1,128]{6,5,4,3,2,1,0:T(1,128)S(1)}, u32[]{:S(2)}, u32[]{:S(2)}) %all-to-all-start) | async-done | bytes 1179680 | tf_op jit(solution)/shard_map/all_to_all | solution.py:127
  135.9 0.8 pad_maximum_fusion.1
  138.0 269.2 %all-reduce.3.cloned.1.call-done = f32[2,4,128,128]{3,2,1,0:T(8,128)} async-done(((f32[2,4,128,128]{3,2,1,0:T(8,128)}), f32[2,4,128,128]{3,2,1,0:T(8,128)}) %all-reduce.3.cloned.1.call-update) | async-done | bytes 524304
  407.3 0.8 constant_dynamic-slice_fusion
  408.3 1.0 reshape.3122
  409.3 51.2 %reduce-scatter.5.cloned.1.call-done = f32[16,32]{1,0:T(8,128)} async-done(((f32[128,32]{1,0:T(8,128)}), f32[16,32]{1,0:T(8,128)}) %reduce-scatter.5.cloned.1.call-update) | async-done | bytes 2064
  460.5 0.8 reshape.3123
  461.4 0.6 broadcast_multiply_fusion
  (182 shorter events, 28.6 us)
Async XLA Ops:
  6.5 7.5 %copy-start = (f32[2,3,4,1,4096]{4,3,2,1,0:T(1,128)S(1)}, f32[2,3,4,1,4096]{4,3,2,1,0:T(1,128)}, u32[]{:S(2)}) copy-start(f32[2,3,4,1,4096]{4,3,2,1,0:T(1,128)} %param.4) | copy-start | bytes 1179652
  6.5 26.0 %collective-permute-start.2 = (f32[2,3,4,1,4096]{4,3,2,1,0:T(1,128)}, f32[2,3,4,1,4096]{4,3,2,1,0:T(1,128)}, u32[]{:S(2)}, u32[]{:S(2)}) collective-permute-start(f32[2,3,4,1,4096]{4,3,2,1,0:T(1,128)} %param.4), channel_id=1, source_target_pairs={{0,32},{32,64},{64,96},{96,128},{128,160},{160,192},{192,224},{224... | collective-permute-start | bytes 1179656 | tf_op jit(solution)/shard_map/ppermute | solution.py:19
  8.1 25.7 %collective-permute-start = (f32[2,3,4,1,4096]{4,3,2,1,0:T(1,128)}, f32[2,3,4,1,4096]{4,3,2,1,0:T(1,128)}, u32[]{:S(2)}, u32[]{:S(2)}) collective-permute-start(f32[2,3,4,1,4096]{4,3,2,1,0:T(1,128)} %param.4), channel_id=1, source_target_pairs={{32,0},{64,32},{96,64},{128,96},{160,128},{192,160},{224,192},{0,2... | collective-permute-start | bytes 1179656 | tf_op jit(solution)/shard_map/ppermute | solution.py:22
  12.8 18.3 %collective-permute-start.1 = (f32[2,3,3,1,4096]{4,3,2,1,0:T(1,128)}, f32[2,3,3,1,4096]{4,3,2,1,0:T(1,128)}, u32[]{:S(2)}, u32[]{:S(2)}) collective-permute-start(f32[2,3,3,1,4096]{4,3,2,1,0:T(1,128)} %get-tuple-element.56), channel_id=1, source_target_pairs={{224,0},{0,32},{32,64},{64,96},{96,128},{128,160},{160,192},{192,2... | collective-permute-start | bytes 884744 | tf_op jit(solution)/shard_map/ppermute | solution.py:30
  15.8 1.2 copy-start.1
  24.3 1.7 copy-start.5
  35.3 0.9 copy-start.2
  35.3 1.0 copy-start.3
  37.8 12.7 %collective-permute-start.4 = (f32[2,3,4,1,4096]{4,2,1,0,3:T(4,128)S(1)}, f32[2,3,4,1,4096]{4,2,1,0,3:T(4,128)S(1)}, u32[]{:S(2)}, u32[]{:S(2)}) collective-permute-start(f32[2,3,4,1,4096]{4,2,1,0,3:T(4,128)S(1)} %fusion.21), channel_id=1, source_target_pairs={{0,32},{32,64},{64,96},{96,128},{128,160},{160,192},{192,224},{224... | collective-permute-start | bytes 1179656 | tf_op jit(solution)/shard_map/ppermute | solution.py:19
  38.6 12.2 %collective-permute-start.3 = (f32[2,3,4,1,4096]{4,2,1,0,3:T(4,128)S(1)}, f32[2,3,4,1,4096]{4,2,1,0,3:T(4,128)S(1)}, u32[]{:S(2)}, u32[]{:S(2)}) collective-permute-start(f32[2,3,4,1,4096]{4,2,1,0,3:T(4,128)S(1)} %fusion.21), channel_id=1, source_target_pairs={{32,0},{64,32},{96,64},{128,96},{160,128},{192,160},{224,192},{0,2... | collective-permute-start | bytes 1179656 | tf_op jit(solution)/shard_map/ppermute | solution.py:22
  53.7 11.9 %collective-permute-start.6 = (f32[2,3,4,1,4096]{4,2,1,0,3:T(4,128)S(1)}, f32[2,3,4,1,4096]{4,2,1,0,3:T(4,128)S(1)}, u32[]{:S(2)}, u32[]{:S(2)}) collective-permute-start(f32[2,3,4,1,4096]{4,2,1,0,3:T(4,128)S(1)} %fusion.28), channel_id=1, source_target_pairs={{0,32},{32,64},{64,96},{96,128},{128,160},{160,192},{192,224},{224... | collective-permute-start | bytes 1179656 | tf_op jit(solution)/shard_map/ppermute | solution.py:19
  54.4 10.5 %collective-permute-start.5 = (f32[2,3,4,1,4096]{4,2,1,0,3:T(4,128)S(1)}, f32[2,3,4,1,4096]{4,2,1,0,3:T(4,128)S(1)}, u32[]{:S(2)}, u32[]{:S(2)}) collective-permute-start(f32[2,3,4,1,4096]{4,2,1,0,3:T(4,128)S(1)} %fusion.28), channel_id=1, source_target_pairs={{32,0},{64,32},{96,64},{128,96},{160,128},{192,160},{224,192},{0,2... | collective-permute-start | bytes 1179656 | tf_op jit(solution)/shard_map/ppermute | solution.py:22
  86.7 11.0 %copy-start.4 = (s32[2,3]{1,0:T(2,128)S(1)}, s32[2,3]{1,0:T(2,128)}, u32[]{:S(2)}) copy-start(s32[2,3]{1,0:T(2,128)} %param.6) | copy-start | bytes 76
  86.7 41.1 %all-to-all-start = ((f32[32,3,2,3,4,1,128]{6,5,4,3,2,1,0:T(1,128)}), f32[32,3,2,3,4,1,128]{6,5,4,3,2,1,0:T(1,128)S(1)}, u32[]{:S(2)}, u32[]{:S(2)}) async-start(f32[32,3,2,3,4,1,128]{6,5,4,3,2,1,0:T(1,128)} %constant_dynamic-update-slice_fusion), calls=%async_computation | async-start | bytes 2359296 | tf_op jit(solution)/shard_map/all_to_all | solution.py:127
  97.6 309.6 %all-reduce.3.cloned.1.call-start = ((), (), s32[]{:S(2)}) async-start(), calls=%async_computation.3 | async-start | bytes 1048576
  135.8 1.0 copy-start.6
  136.7 323.8 %reduce-scatter.5.cloned.1.call-start = ((), (), s32[]{:S(2)}) async-start(), calls=%async_computation.2 | async-start | bytes 73728
Sparse Core Ops, SparseCore 0:
  136.9 270.3 all-reduce.2
  409.9 50.5 reduce-scatter.4
